TPU v7x, 32 devices: a whole 2x2x4 slice. The times are simulated.
32 devices in a mesh: dp: 8 (over y, x, core), fsdp: 4 (over z).
Axes of the slice: x: 2, y: 2, z: 4, core: 2. Of those that a mesh axis runs over, the one named last changes fastest.
Arguments:
- glu_frames: bfloat16 [8192, 1536], P(('dp', 'fsdp')), may hold values from -6 to 6
- residual_frames: bfloat16 [8192, 1536], P(('dp', 'fsdp')), may hold values from -6 to 6
- send_rows: int32 [8, 4, 8, 32], P('dp', 'fsdp'), may hold values from 0 to 255, as said below
- recv_slot: int32 [8, 4, 128], P('dp', 'fsdp'), may hold values from 0 to 255, as said below
- segment_ids: int32 [8, 4, 128], P('dp', 'fsdp'), may hold values from 0 to 15, never falling along the last dimension, each value on 1 to 64 neighbouring positions
- code_targets: int32 [8, 512], P('dp'), may hold values from 0 to 8191
- conv_kernel: float32 [31, 1536], replicated, may hold values from -1 to 1
- norm_gain: float32 [1536], replicated, may hold values from 0.5 to 1.5
- point_weight: bfloat16 [1536, 1536], P('fsdp'), may hold values from -0.15625 to 0.15625
- code_head: bfloat16 [1536, 8192], P(None, 'fsdp')
Outputs:
- loss: float32 [], replicated
- grad_head: float32 [1536, 8192], P('dp', 'fsdp')
- grad_point: float32 [1536, 1536], P('fsdp', 'dp')
- grad_kernel: float32 [31, 1536], replicated
- grad_gain: float32 [1536], replicated
- grad_residual: bfloat16 [4096, 1536], P(('dp', 'fsdp'))
- grad_glu: bfloat16 [4096, 1536], P(('dp', 'fsdp'))
Inputs may be any that keep to these rules, and one draw needn't show every extreme that they name: send_rows[i, f, o] lists 32 local slots of loading device (i, f) for owner (o, f). Each loading device fills whole buckets for between 2 and 8 owners, at most one bucket per owner, with distinct slots; its entries for other owners are never read. recv_slot[o, f, r] = i * 32 + c names position c of the bucket from loading device (i, f). Each owner reads 4 full buckets of 32 frames, from distinct loading devices, each whole and in order.
All inputs are finite; a program needn't handle non-finite values.
Results may differ from a plain program's by a relative error of at most 0.012.
The roundings to bfloat16 on the way count: a program that leaves them out, or rounds other values in their place, can miss the bound.
Values may be sent and summed in bfloat16 or wider, within the bound.
No kernel may reach another device: no remote copies, remote signals or barrier semaphores. Data moves between devices by JAX's collectives and lax.ppermute only.
A program may use at most 128 MiB of HBM per device.

v0:
```python
import jax
import jax.numpy as jnp
from jax import lax
from jax.sharding import PartitionSpec as P


def merged(value, axis, join):
    pieces = jax.tree.map(lambda part: lax.all_gather(part, axis), value)
    head = jax.tree.map(lambda part: part[0], pieces)
    tail = jax.tree.map(lambda part: part[1:], pieces)
    subtotal, _ = lax.scan(lambda subtotal, share: (join(subtotal, share), None), head, tail)
    return subtotal


def join_softmax(former, latter):
    joined_top = jnp.maximum(former[0], latter[0])
    joined_sum = former[1] * jnp.exp(former[0] - joined_top) + latter[1] * jnp.exp(
        latter[0] - joined_top
    )
    return (joined_top, joined_sum)


def local(
    glu_frames,
    residual_frames,
    send_rows,
    recv_slot,
    segment_ids,
    code_targets,
    conv_kernel,
    norm_gain,
    point_weight,
    code_head,
):
    feature_width = glu_frames.shape[1]
    tap_count = conv_kernel.shape[0]
    half_taps = tap_count // 2
    slot_list = recv_slot[0, 0]
    row_count = slot_list.shape[0]
    picked_rows = send_rows[0, 0]
    glu_sent = glu_frames[picked_rows]
    residual_sent = residual_frames[picked_rows]
    glu_recv, residual_recv = (
        lax.all_to_all(glu_sent, "dp", split_axis=0, concat_axis=0, tiled=True),
        lax.all_to_all(residual_sent, "dp", split_axis=0, concat_axis=0, tiled=True),
    )
    glu_owned = glu_recv.reshape(-1, feature_width)[slot_list]
    residual_owned = residual_recv.reshape(-1, feature_width)[slot_list]
    segments = segment_ids[0, 0]
    seg_pad = jnp.pad(segments, (half_taps, half_taps), constant_values=-1)
    glu_pad = jnp.pad(glu_owned.astype(jnp.float32), ((half_taps, half_taps), (0, 0)))
    conv_out = jnp.zeros((row_count, feature_width), jnp.float32)
    kept_list = []
    for offset in range(tap_count):
        same_seg = (seg_pad[offset : offset + row_count] == segments)[:, None]
        kept = jnp.where(same_seg, glu_pad[offset : offset + row_count], 0.0)
        kept_list.append(kept)
        conv_out = conv_out + conv_kernel[offset] * kept
    centred = conv_out - jnp.mean(conv_out, axis=1, keepdims=True)
    inv_std = lax.rsqrt(jnp.mean(centred * centred, axis=1, keepdims=True) + 1e-05)
    standard = centred * inv_std
    normed = standard * norm_gain
    gate_sig = jax.nn.sigmoid(normed)
    activation = (normed * gate_sig).astype(jnp.bfloat16)
    full_panel = lax.all_gather(point_weight, "fsdp", axis=0, tiled=True)
    branch_out = jnp.dot(activation, full_panel, preferred_element_type=jnp.float32)
    residual_new = (residual_owned.astype(jnp.float32) + branch_out).astype(jnp.bfloat16)
    group_rows = lax.all_gather(residual_new, "fsdp", axis=0, tiled=True)
    logits = jnp.dot(group_rows, code_head, preferred_element_type=jnp.float32)
    code_local = code_head.shape[1]
    fsdp_index = lax.axis_index("fsdp")
    local_target = code_targets[0] - fsdp_index * code_local
    target_hits = local_target[:, None] == lax.broadcasted_iota(jnp.int32, (1, code_local), 1)
    row_top = jnp.max(logits, axis=1)
    row_sum = jnp.sum(jnp.exp(logits - row_top[:, None]), axis=1)
    pick_total = jnp.sum(jnp.where(target_hits, logits, 0.0))
    merged_top, merged_sum = merged((row_top, row_sum), "fsdp", join_softmax)
    log_norm = merged_top + jnp.log(merged_sum)
    loss_part = (
        jnp.sum(lax.dynamic_slice_in_dim(log_norm, fsdp_index * row_count, row_count, 0))
        - pick_total
    )
    logit_grad = (jnp.exp(logits - log_norm[:, None]) - target_hits.astype(jnp.float32)).astype(
        jnp.bfloat16
    )
    head_local = lax.dot_general(
        group_rows, logit_grad, (((0,), (0,)), ((), ())), preferred_element_type=jnp.float32
    )
    grad_head = lax.psum_scatter(
        head_local.astype(jnp.bfloat16), "dp", scatter_dimension=0, tiled=True
    ).astype(jnp.float32)
    grad_residual = lax.psum_scatter(
        lax.dot_general(
            logit_grad, code_head, (((1,), (1,)), ((), ())), preferred_element_type=jnp.float32
        ),
        "fsdp",
        scatter_dimension=0,
        tiled=True,
    ).astype(jnp.bfloat16)
    whole_grad = lax.dot_general(
        activation, grad_residual, (((0,), (0,)), ((), ())), preferred_element_type=jnp.float32
    )
    column_sum = lax.psum_scatter(
        whole_grad.astype(jnp.bfloat16), "dp", scatter_dimension=1, tiled=True
    )
    grad_point = lax.psum_scatter(column_sum, "fsdp", scatter_dimension=0, tiled=True).astype(
        jnp.float32
    )
    act_grad = lax.dot_general(
        grad_residual, full_panel, (((1,), (1,)), ((), ())), preferred_element_type=jnp.float32
    )
    normed_grad = act_grad * gate_sig * (1.0 + normed * (1.0 - gate_sig))
    gain_grad = jnp.sum(normed_grad * standard, axis=0)
    scaled = normed_grad * norm_gain
    conv_grad = inv_std * (
        scaled
        - jnp.mean(scaled, axis=1, keepdims=True)
        - standard * jnp.mean(scaled * standard, axis=1, keepdims=True)
    )
    kernel_grad = jnp.stack([jnp.sum(conv_grad * kept, axis=0) for kept in kept_list])
    grad_pad = jnp.pad(conv_grad, ((half_taps, half_taps), (0, 0)))
    glu_grad = jnp.zeros((row_count, feature_width), jnp.float32)
    for offset in range(tap_count):
        begin_row = 2 * half_taps - offset
        same_seg = (seg_pad[begin_row : begin_row + row_count] == segments)[:, None]
        glu_grad = glu_grad + conv_kernel[offset] * jnp.where(
            same_seg, grad_pad[begin_row : begin_row + row_count], 0.0
        )
    loss_sum, kernel_sum, gain_sum = lax.psum((loss_part, kernel_grad, gain_grad), ("dp", "fsdp"))
    loss = loss_sum / (row_count * lax.axis_size("dp") * lax.axis_size("fsdp"))
    return (
        loss,
        grad_head,
        grad_point,
        kernel_sum,
        gain_sum,
        grad_residual,
        glu_grad.astype(jnp.bfloat16),
    )


def solution(mesh):
    placed = (
        P(("dp", "fsdp"), None),
        P(("dp", "fsdp"), None),
        P("dp", "fsdp", None, None),
        P("dp", "fsdp", None),
        P("dp", "fsdp", None),
        P("dp", None),
        P(),
        P(),
        P("fsdp", None),
        P(None, "fsdp"),
    )
    return jax.shard_map(
        local,
        mesh=mesh,
        in_specs=placed,
        out_specs=(
            P(),
            P("dp", "fsdp"),
            P("fsdp", "dp"),
            P(),
            P(),
            P(("dp", "fsdp"), None),
            P(("dp", "fsdp"), None),
        ),
        check_vma=False,
    )
```

profile of v0, /device:TPU:0, one launch (start us, length us, event | category | flops | bytes accessed | tf_op | source)
XLA Modules:
  0.0 533.4 jit_solution(17724211208006265354)
XLA Ops:
  10.9 5.3 all-to-all-start.1
  18.7 10.1 %all-to-all-done.1 = bf16[8,32,1536]{2,1,0:T(8,128)(2,1)S(1)} async-done(((bf16[8,32,1536]{2,1,0:T(8,128)(2,1)}), bf16[8,32,1536]{2,1,0:T(8,128)(2,1)S(1)}, u32[]{:S(2)}, u32[]{:S(2)}) %all-to-all-start.1) | async-done | bytes 786464 | tf_op jit(solution)/shard_map/all_to_all | solution.py:44
  28.8 3.5 all-to-all-start
  35.3 9.6 %all-to-all-done = bf16[8,32,1536]{2,1,0:T(8,128)(2,1)S(1)} async-done(((bf16[8,32,1536]{2,1,0:T(8,128)(2,1)}), bf16[8,32,1536]{2,1,0:T(8,128)(2,1)S(1)}, u32[]{:S(2)}, u32[]{:S(2)}) %all-to-all-start) | async-done | bytes 786464 | tf_op jit(solution)/shard_map/all_to_all | solution.py:45
  46.1 5.2 fusion.155
  51.7 50.0 %all-gather.7.cloned.1.call-done = bf16[1536,1536]{1,0:T(8,128)(2,1)} async-done(((bf16[384,1536]{1,0:T(8,128)(2,1)}), bf16[1536,1536]{1,0:T(8,128)(2,1)}) %all-gather.7.cloned.1.call-update) | async-done | bytes 4718608 | tf_op jit(solution)/shard_map/all_gather | solution.py:65
  101.7 4.0 fusion.1
  106.0 35.4 %all-gather.9.cloned.1.call-done = bf16[512,1536]{1,0:T(8,128)(2,1)} async-done(((bf16[128,1536]{1,0:T(8,128)(2,1)}), bf16[512,1536]{1,0:T(8,128)(2,1)}) %all-gather.9.cloned.1.call-update) | async-done | bytes 1572880 | tf_op jit(solution)/shard_map/all_gather | solution.py:68
  141.4 6.1 %fusion.156 = (f32[512]{0:T(512)S(1)}, f32[512,2048]{1,0:T(8,128)S(1)}) fusion(bf16[512,1536]{1,0:T(8,128)(2,1)} %all-gather.9.cloned.1.call-done, bf16[1536,2048]{1,0:T(8,128)(2,1)} %param.21), kind=kOutput, calls=%fused_computation.345 | convolution fusion | flops 3222273536 | bytes 12060672 | tf_op jit(solution)/shard_map/dot_general | solution.py:69
  149.6 2.9 select_reduce_fusion
  152.5 11.9 %all-gather.3 = f32[4,1,512]{2,1,0:T(1,128)S(1)} all-gather(f32[1,1,512]{2,1,0:T(1,128)S(1)} %bitcast.48), channel_id=3, replica_groups=mesh['dp'=8,'fsdp'=4] {'fsdp'}, dimensions={0}, use_global_device_ids=true | all-gather | bytes 10240 | tf_op jit(solution)/shard_map/all_gather | solution.py:8
  164.3 11.9 %all-gather.2 = f32[4,1,512]{2,1,0:T(1,128)S(1)} all-gather(f32[1,1,512]{2,1,0:T(1,128)S(1)} %bitcast.47), channel_id=2, replica_groups=mesh['dp'=8,'fsdp'=4] {'fsdp'}, dimensions={0}, use_global_device_ids=true | all-gather | bytes 10240 | tf_op jit(solution)/shard_map/all_gather | solution.py:8
  176.4 9.3 %fusion.154 = f32[512,1536]{1,0:T(8,128)} fusion(bf16[1536,2048]{1,0:T(8,128)(2,1)} %param.21, f32[512,2048]{1,0:T(8,128)} %copy-done.2, f32[512]{0:T(512)S(1)} %log_add_fusion, s32[512]{0:T(512)S(1)} %bitcast.50), kind=kOutput, calls=%fused_computation.343 | convolution fusion | flops 3226468352 | bytes 13635584 | tf_op jit(solution)/shard_map/dot_general | solution.py:93
  185.8 58.9 %reduce-scatter.9.cloned.1.call-done = f32[128,1536]{1,0:T(8,128)} async-done(((f32[512,1536]{1,0:T(8,128)}), f32[128,1536]{1,0:T(8,128)}) %reduce-scatter.9.cloned.1.call-update) | async-done | bytes 786448 | tf_op jit(solution)/shard_map/reduce_scatter | solution.py:92
  245.8 3.8 convolution_convert_fusion.1
  249.7 9.3 %convolution_convert_fusion = bf16[1536,2048]{1,0:T(8,128)(2,1)} fusion(bf16[512,1536]{1,0:T(8,128)(2,1)} %all-gather.9.cloned.1.call-done, f32[512,2048]{1,0:T(8,128)} %copy-done.2, f32[512]{0:T(512)S(1)} %log_add_fusion, s32[512]{0:T(512)S(1)} %bitcast.51), kind=kOutput, calls=%fused_computation.7 | convolution fusion | flops 3229614080 | bytes 12062720 | tf_op jit(solution)/shard_map/dot_general | solution.py:86
  261.3 6.0 %multiply_reduce_fusion = (f32[1536]{0:T(1024)}, f32[128]{0:T(128)S(1)}, f32[128]{0:T(128)S(1)}, f32[128,1536]{1,0:T(8,128)}) fusion(f32[128,1536]{1,0:T(8,128)S(1)} %get-tuple-element.120, f32[128]{0:T(128)S(1)} %add_rsqrt_fusion, f32[128]{0:T(128)S(1)} %broadcast_multiply_fusion.2, f32[1536]{0:T(1024)S(1)} %copy-done.5, ...), kind=kOutput, calls=%fused_computation.198 | convolution fusion | flops 607320320 | bytes 6699008 | tf_op jit(solution)/shard_map/dot_general | solution.py:109
  267.8 35.9 %reduce-scatter.11.cloned.1.call-done = bf16[1536,192]{0,1:T(8,128)(2,1)} async-done(((bf16[1536,1536]{0,1:T(8,128)(2,1)}), bf16[1536,192]{0,1:T(8,128)(2,1)}) %reduce-scatter.11.cloned.1.call-update) | async-done | bytes 589840 | tf_op jit(solution)/shard_map/reduce_scatter | solution.py:103
  306.0 3.0 multiply_reduce_fusion.1
  319.0 6.3 %fusion.108 = bf16[128,1536]{1,0:T(8,128)(2,1)} fusion(f32[128,1536]{1,0:T(8,128)S(1)} %get-tuple-element.118, f32[1536]{0:T(1024)S(1)} %copy-done.63, f32[1536]{0:T(1024)S(1)} %copy-done.65, f32[1536]{0:T(1024)S(1)} %copy-done.7, f32[1536]{0:T(1024)S(1)} %copy-done.9, f32[1536]{0:T(1024)S(1)} %copy-done.11, f32[1536]{0:T(1024)S(1)} %copy-done.13, ...), kind=kLoop, calls=%fused_computation.183 | loop fusion | flops 18087936 | bytes 1373952 | tf_op jit(solution)/shard_map/convert_element_type | solution.py:138
  325.2 39.9 %all-reduce.3 = (f32[]{:T(128)}, f32[1536]{0:T(1024)}) all-reduce(f32[]{:T(128)S(6)} %sub.70, f32[1536]{0:T(1024)S(1)} %copy-done.85), channel_id=1, replica_groups=mesh['dp'=8,'fsdp'=4] {'dp','fsdp'}, use_global_device_ids=true, to_apply=%region_8.9 | all-reduce | flops 1537 | bytes 12296 | tf_op jit(solution)/shard_map/psum | solution.py:129
  365.8 4.3 reduce-scatter.7.cloned.1.call-done
  372.5 22.9 %reduce-scatter.13.cloned.1.call-done = bf16[384,192]{1,0:T(8,128)(2,1)} async-done(((bf16[1536,192]{1,0:T(8,128)(2,1)}), bf16[384,192]{1,0:T(8,128)(2,1)}) %reduce-scatter.13.cloned.1.call-update) | async-done | bytes 147472
  397.2 126.6 %all-reduce.6.cloned.1.call-done = f32[31,1536]{1,0:T(8,128)} async-done(((f32[31,1536]{1,0:T(8,128)}), f32[31,1536]{1,0:T(8,128)}) %all-reduce.6.cloned.1.call-update) | async-done | bytes 190480 | tf_op jit(solution)/shard_map/psum | solution.py:129
  (269 shorter events, 32.5 us)
Async XLA Ops:
  7.2 94.5 %all-gather.7.cloned.1.call-start = ((), (), s32[]{:S(2)}) async-start(), calls=%async_computation.6 | async-start | bytes 5898240 | tf_op jit(solution)/shard_map/all_gather | solution.py:65
  10.9 17.9 %all-to-all-start.1 = ((bf16[8,32,1536]{2,1,0:T(8,128)(2,1)}), bf16[8,32,1536]{2,1,0:T(8,128)(2,1)S(1)}, u32[]{:S(2)}, u32[]{:S(2)}) async-start(bf16[8,32,1536]{2,1,0:T(8,128)(2,1)} %bitcast.8), calls=%async_computation.1 | async-start | bytes 1572864 | tf_op jit(solution)/shard_map/all_to_all | solution.py:44
  18.5 27.3 %copy-start.42 = (f32[1536]{0:T(1024)}, f32[1536]{0:T(1024)S(1)}, u32[]{:S(2)}) copy-start(f32[1536]{0:T(1024)S(1)} %get-tuple-element.92) | copy-start | bytes 18436
  18.5 27.3 %copy-start.44 = (f32[1536]{0:T(1024)}, f32[1536]{0:T(1024)S(1)}, u32[]{:S(2)}) copy-start(f32[1536]{0:T(1024)S(1)} %get-tuple-element.93) | copy-start | bytes 18436
  18.5 27.3 %copy-start.46 = (f32[1536]{0:T(1024)}, f32[1536]{0:T(1024)S(1)}, u32[]{:S(2)}) copy-start(f32[1536]{0:T(1024)S(1)} %get-tuple-element.94) | copy-start | bytes 18436
  18.6 27.3 %copy-start.48 = (f32[1536]{0:T(1024)}, f32[1536]{0:T(1024)S(1)}, u32[]{:S(2)}) copy-start(f32[1536]{0:T(1024)S(1)} %get-tuple-element.95) | copy-start | bytes 18436
  18.6 27.3 %copy-start.50 = (f32[1536]{0:T(1024)}, f32[1536]{0:T(1024)S(1)}, u32[]{:S(2)}) copy-start(f32[1536]{0:T(1024)S(1)} %get-tuple-element.96) | copy-start | bytes 18436
  18.6 27.3 %copy-start.52 = (f32[1536]{0:T(1024)}, f32[1536]{0:T(1024)S(1)}, u32[]{:S(2)}) copy-start(f32[1536]{0:T(1024)S(1)} %get-tuple-element.97) | copy-start | bytes 18436
  18.6 27.3 %copy-start.54 = (f32[1536]{0:T(1024)}, f32[1536]{0:T(1024)S(1)}, u32[]{:S(2)}) copy-start(f32[1536]{0:T(1024)S(1)} %get-tuple-element.98) | copy-start | bytes 18436
  18.6 27.3 %copy-start.56 = (f32[1536]{0:T(1024)}, f32[1536]{0:T(1024)S(1)}, u32[]{:S(2)}) copy-start(f32[1536]{0:T(1024)S(1)} %get-tuple-element.99) | copy-start | bytes 18436
  18.6 27.3 %copy-start.58 = (f32[1536]{0:T(1024)}, f32[1536]{0:T(1024)S(1)}, u32[]{:S(2)}) copy-start(f32[1536]{0:T(1024)S(1)} %get-tuple-element.100) | copy-start | bytes 18436
  18.6 27.3 %copy-start.60 = (f32[1536]{0:T(1024)}, f32[1536]{0:T(1024)S(1)}, u32[]{:S(2)}) copy-start(f32[1536]{0:T(1024)S(1)} %get-tuple-element.101) | copy-start | bytes 18436
  18.6 27.3 %copy-start.62 = (f32[1536]{0:T(1024)}, f32[1536]{0:T(1024)S(1)}, u32[]{:S(2)}) copy-start(f32[1536]{0:T(1024)S(1)} %get-tuple-element.102) | copy-start | bytes 18436
  28.8 16.1 %all-to-all-start = ((bf16[8,32,1536]{2,1,0:T(8,128)(2,1)}), bf16[8,32,1536]{2,1,0:T(8,128)(2,1)S(1)}, u32[]{:S(2)}, u32[]{:S(2)}) async-start(bf16[8,32,1536]{2,1,0:T(8,128)(2,1)} %bitcast.3), calls=%async_computation | async-start | bytes 1572864 | tf_op jit(solution)/shard_map/all_to_all | solution.py:45
  32.3 109.1 %all-gather.9.cloned.1.call-start = ((), (), s32[]{:S(2)}) async-start(), calls=%async_computation.7 | async-start | bytes 1966080 | tf_op jit(solution)/shard_map/all_gather | solution.py:68
  35.3 66.5 %copy-start.5 = (f32[1536]{0:T(1024)S(1)}, f32[1536]{0:T(1024)}, u32[]{:S(2)}) copy-start(f32[1536]{0:T(1024)} %param.19) | copy-start | bytes 18436
  51.4 209.8 %copy-start.84 = (f32[128]{0:T(128)}, f32[128]{0:T(128)S(1)}, u32[]{:S(2)}) copy-start(f32[128]{0:T(128)S(1)} %broadcast_multiply_fusion.2) | copy-start | bytes 1540
  51.7 209.6 %copy-start.86 = (f32[128]{0:T(128)}, f32[128]{0:T(128)S(1)}, u32[]{:S(2)}) copy-start(f32[128]{0:T(128)S(1)} %add_rsqrt_fusion) | copy-start | bytes 1540
  51.7 54.3 %copy-start.87 = (s32[1,512]{1,0:T(1,128)S(1)}, s32[1,512]{1,0:T(1,128)}, u32[]{:S(2)}) copy-start(s32[1,512]{1,0:T(1,128)} %param.17) | copy-start | bytes 6148
  105.7 138.9 %reduce-scatter.9.cloned.1.call-start = ((), (), s32[]{:S(2)}) async-start(), calls=%async_computation.9 | async-start | bytes 3932160 | tf_op jit(solution)/shard_map/reduce_scatter | solution.py:92
  185.7 118.0 %reduce-scatter.11.cloned.1.call-start = ((), (), s32[]{:S(2)}) async-start(), calls=%async_computation.10 | async-start | bytes 5308416 | tf_op jit(solution)/shard_map/reduce_scatter | solution.py:103
  249.6 120.4 %reduce-scatter.7.cloned.1.call-start = ((), (), s32[]{:S(2)}) async-start(), calls=%async_computation.8 | async-start | bytes 7077888 | tf_op jit(solution)/shard_map/reduce_scatter | solution.py:89
  259.0 136.4 %reduce-scatter.13.cloned.1.call-start = ((), (), s32[]{:S(2)}) async-start(), calls=%async_computation.12 | async-start | bytes 983040
  305.9 217.9 %all-reduce.6.cloned.1.call-start = ((), (), s32[]{:S(2)}) async-start(), calls=%async_computation.11 | async-start | bytes 393216 | tf_op jit(solution)/shard_map/psum | solution.py:129
  (75 other events, 864.0 us)
Sparse Core Ops, SparseCore 0:
  9.6 92.0 all-gather.6
  105.9 35.5 all-gather.8
  185.8 58.7 reduce-scatter.8
  249.8 53.8 reduce-scatter.10
  307.3 62.6 reduce-scatter.6
  372.2 23.1 reduce-scatter.12
  401.5 122.2 all-reduce.5
where the time goes:
time: 534 us; the launch traced here: 533 us
  waiting for transfers between devices  355 us (66%)
  blocking collectives  63.6 us (12%)
  matrix products  38.5 us (7%)
  other arithmetic  31.3 us (6%)
  between operations  19 us (4%)
  local copies, waits for them, and re-layouts  16.9 us (3%)
  starting transfers between devices  9.54 us (2%)
    psum x1, waiting for transfers between devices, local(): lax.psum((loss_part, kernel_grad, gain_grad), ('dp', 'fsdp'))  127 us
    reduce_scatter x1, waiting for transfers between devices, local(): lax.psum_scatter(lax.dot_general(logit_grad, code_head, (((1,), (1,)), ((...  58.9 us
    all_gather x1, waiting for transfers between devices, local(): full_panel = lax.all_gather(point_weight, 'fsdp', axis=0, tiled=True)  50 us
    psum x1, blocking collectives, local(): lax.psum((loss_part, kernel_grad, gain_grad), ('dp', 'fsdp'))  39.9 us
    reduce_scatter x1, waiting for transfers between devices, local(): lax.psum_scatter(whole_grad.astype(jnp.bfloat16), 'dp', scatter_dimension...  35.9 us
    all_gather x1, waiting for transfers between devices, local(): group_rows = lax.all_gather(residual_new, 'fsdp', axis=0, tiled=True)  35.4 us
    unnamed x8, waiting for transfers between devices  23.7 us
    all_gather x2, blocking collectives, merged(): pieces = jax.tree.map(lambda part: lax.all_gather(part, axis), value)  23.7 us
  transfers between devices with their start and end apart: 9, of which 9 were waited for; matrix products, arithmetic and copies ran while one was open for 10% of the time, Pallas kernels for 0%

commit v1 on v0

v1 whole, which is shorter than its diff:
```python
import jax
import jax.numpy as jnp
from jax import lax
from jax.sharding import PartitionSpec as P

F32 = jnp.float32
BF16 = jnp.bfloat16


def flip_dp(value, mask):
    count = lax.axis_size("dp")
    return lax.ppermute(value, "dp", [(i, i ^ mask) for i in range(count)])


def flip_fsdp(value, mask):
    count = lax.axis_size("fsdp")
    return lax.ppermute(value, "fsdp", [(i, i ^ mask) for i in range(count)])


def shift_fsdp(value, step):
    count = lax.axis_size("fsdp")
    return lax.ppermute(value, "fsdp", [(i, (i + step) % count) for i in range(count)])


def pick(array, index, axis=0):
    return lax.dynamic_index_in_dim(array, index, axis, keepdims=False)


def ordered(bit, own, other, axis):
    return jnp.where(
        bit == 0, jnp.stack([own, other], axis), jnp.stack([other, own], axis)
    )


def tree_sum(values):
    while len(values) > 1:
        values = [values[i] + values[i + 1] for i in range(0, len(values), 2)]
    return values[0]


def gather_point(point_weight, d, f):
    count = lax.axis_size("fsdp")
    rows, width = point_weight.shape
    core, bit1, bit2 = d & 1, (d >> 1) & 1, (d >> 2) & 1
    parts = point_weight.reshape(2, 2, 2, rows // 8, width)
    piece1 = pick(pick(parts[0], bit1), core)
    piece2 = pick(pick(parts[1], bit2), core)
    piece = jnp.stack([piece1, piece2])
    got = jnp.stack([shift_fsdp(piece, step) for step in range(1, count)])
    first, second = got[:, 0], got[:, 1]
    half1 = ordered(bit1, first, flip_dp(first, 2), 1)
    half2 = ordered(bit2, second, flip_dp(second, 4), 1)
    mine = jnp.stack([half1, half2], 1)
    whole = ordered(core, mine, flip_dp(mine, 1), 3).reshape(count - 1, rows, width)
    panel = jnp.zeros((count, rows, width), point_weight.dtype)
    panel = lax.dynamic_update_index_in_dim(panel, point_weight, f, 0)
    for step in range(1, count):
        panel = lax.dynamic_update_index_in_dim(panel, whole[step - 1], (f - step) % count, 0)
    return panel.reshape(count * rows, width)


def gather_rows(own, f):
    count = lax.axis_size("fsdp")
    if count != 4:
        return [(0, own)] + [(count - step, shift_fsdp(own, step)) for step in range(1, count)]
    before = shift_fsdp(own, 1)
    after = shift_fsdp(own, -1)
    source = jnp.where(f == 2, before, jnp.where(f == 1, after, own))
    across = lax.ppermute(source, "fsdp", [(0, 2), (3, 1), (2, 3), (1, 0)])
    return [(0, own), (3, before), (1, after), (2, across)]


def scatter_rows(blocks, f):
    count = lax.axis_size("fsdp")
    if count != 4:
        total = blocks[0]()
        for step in range(1, count):
            total = total + shift_fsdp(blocks[step]().astype(BF16), step).astype(F32)
        return total
    across = lax.ppermute(
        blocks[2]().astype(BF16), "fsdp", [(2, 0), (1, 3), (3, 2), (0, 1)]
    ).astype(F32)
    ahead, behind = blocks[1](), blocks[3]()
    ahead = ahead + jnp.where(f == 1, across, 0.0)
    behind = behind + jnp.where(f == 2, across, 0.0)
    got1 = shift_fsdp(ahead.astype(BF16), 1).astype(F32)
    got2 = shift_fsdp(behind.astype(BF16), -1).astype(F32)
    direct = jnp.where((f == 0) | (f == 3), across, 0.0)
    return blocks[0]() + direct + got1 + got2


def reduce_head(head, d):
    count = lax.axis_size("dp")
    bits = count.bit_length() - 1
    rows, width = head.shape
    cut = head.reshape(*([2] * bits), rows // count, width)

    def halve(value, left, bit):
        axis = left.index(bit)
        mine = (d >> bit) & 1
        sent = flip_dp(pick(value, 1 - mine, axis), 1 << bit)
        total = pick(value, mine, axis).astype(F32) + sent.astype(F32)
        return total, [b for b in left if b != bit]

    left = list(range(bits - 1, -1, -1))
    total, left = halve(cut, left, 0)
    total = total.astype(BF16)
    half = width // 2
    sides = [(total[..., :half], left), (total[..., half:], left)]
    orders = [list(range(1, bits)), list(range(bits - 1, 0, -1))]
    for step in range(bits - 1):
        sides = [halve(v.astype(BF16), l, o[step]) for (v, l), o in zip(sides, orders)]
    return jnp.concatenate([v for v, _ in sides], axis=-1)


def local(
    glu_frames,
    residual_frames,
    send_rows,
    recv_slot,
    segment_ids,
    code_targets,
    conv_kernel,
    norm_gain,
    point_weight,
    code_head,
):
    n_dp, n_fsdp = lax.axis_size("dp"), lax.axis_size("fsdp")
    d, f = lax.axis_index("dp"), lax.axis_index("fsdp")
    feature_width = glu_frames.shape[1]
    tap_count = conv_kernel.shape[0]
    half_taps = tap_count // 2
    slot_list = recv_slot[0, 0]
    row_count = slot_list.shape[0]
    picked_rows = send_rows[0, 0]

    glu_sent = glu_frames[picked_rows]
    glu_recv = lax.all_to_all(glu_sent, "dp", split_axis=0, concat_axis=0, tiled=True)
    full_panel = gather_point(point_weight, d, f)
    residual_sent = residual_frames[picked_rows]
    residual_recv = lax.all_to_all(residual_sent, "dp", split_axis=0, concat_axis=0, tiled=True)

    glu_owned = glu_recv.reshape(-1, feature_width)[slot_list]
    residual_owned = residual_recv.reshape(-1, feature_width)[slot_list]
    segments = segment_ids[0, 0]
    seg_pad = jnp.pad(segments, (half_taps, half_taps), constant_values=-1)
    glu_pad = jnp.pad(glu_owned.astype(F32), ((half_taps, half_taps), (0, 0)))
    conv_out = jnp.zeros((row_count, feature_width), F32)
    kept_list = []
    for offset in range(tap_count):
        same_seg = (seg_pad[offset : offset + row_count] == segments)[:, None]
        kept = jnp.where(same_seg, glu_pad[offset : offset + row_count], 0.0)
        kept_list.append(kept)
        conv_out = conv_out + conv_kernel[offset] * kept
    centred = conv_out - jnp.mean(conv_out, axis=1, keepdims=True)
    inv_std = lax.rsqrt(jnp.mean(centred * centred, axis=1, keepdims=True) + 1e-05)
    standard = centred * inv_std
    normed = standard * norm_gain
    gate_sig = jax.nn.sigmoid(normed)
    activation = (normed * gate_sig).astype(BF16)

    branch_out = jnp.dot(activation, full_panel, preferred_element_type=F32)
    residual_new = (residual_owned.astype(F32) + branch_out).astype(BF16)

    code_local = code_head.shape[1]
    targets = code_targets[0].reshape(n_fsdp, row_count) - f * code_local
    columns = lax.broadcasted_iota(jnp.int32, (1, code_local), 1)
    gathered = gather_rows(residual_new, f)
    logits, hits, stats = {}, {}, {}
    for distance, block in gathered:
        logits[distance] = jnp.dot(block, code_head, preferred_element_type=F32)
        hits[distance] = pick(targets, (f + distance) % n_fsdp)[:, None] == columns
        top = jnp.max(logits[distance], axis=1)
        total = jnp.sum(jnp.exp(logits[distance] - top[:, None]), axis=1)
        chosen = jnp.sum(jnp.where(hits[distance], logits[distance], 0.0), axis=1)
        stats[distance] = jnp.stack([top, total, chosen])
    act_even = [activation] + [flip_dp(activation, mask) for mask in range(2, n_dp, 2)]
    act_even = jnp.concatenate(act_even)
    act_odd = flip_dp(act_even, 1)
    table = jnp.zeros((n_fsdp, 3, row_count), F32)
    for distance, _ in gathered:
        table = lax.dynamic_update_index_in_dim(
            table, stats[distance], (f + distance) % n_fsdp, 0
        )
    tables = [table] + [flip_fsdp(table, mask) for mask in range(1, n_fsdp)]
    tops = tables[0][:, 0]
    for other in tables[1:]:
        tops = jnp.maximum(tops, other[:, 0])
    sums = tree_sum([t[:, 1] * jnp.exp(t[:, 0] - tops) for t in tables])
    log_norm = tops + jnp.log(sums)
    loss_part = jnp.sum(log_norm - tree_sum([t[:, 2] for t in tables]))

    def logit_grad(distance):
        norm = pick(log_norm, (f + distance) % n_fsdp)[:, None]
        return (jnp.exp(logits[distance] - norm) - hits[distance].astype(F32)).astype(BF16)

    grads = {distance: logit_grad(distance) for distance, _ in gathered}

    def row_grad(distance):
        return lambda: lax.dot_general(
            grads[distance], code_head, (((1,), (1,)), ((), ())), preferred_element_type=F32
        )

    grad_residual = scatter_rows(
        {distance: row_grad(distance) for distance, _ in gathered}, f
    ).astype(BF16)

    all_rows = jnp.concatenate([block for _, block in gathered])
    all_grads = jnp.concatenate([grads[distance] for distance, _ in gathered])
    head_local = lax.dot_general(
        all_rows, all_grads, (((0,), (0,)), ((), ())), preferred_element_type=F32
    ).astype(BF16)
    grad_head = reduce_head(head_local, d)

    part_width = feature_width // n_dp
    cols = lax.all_to_all(
        grad_residual.reshape(row_count, n_dp, part_width).transpose(1, 0, 2),
        "dp",
        split_axis=0,
        concat_axis=0,
        tiled=True,
    )
    bits = n_dp.bit_length() - 1
    cols = cols.reshape(*([2] * bits), row_count, part_width)
    for bit in range(bits):
        axis = bits - 1 - bit
        cols = jnp.where((d >> bit) & 1 == 1, jnp.flip(cols, axis), cols)
    cols = jnp.moveaxis(cols, bits - 1, 0)
    act_all = jnp.concatenate([act_even, act_odd])
    point_part = lax.dot_general(
        act_all,
        cols.reshape(n_dp * row_count, part_width),
        (((0,), (0,)), ((), ())),
        preferred_element_type=F32,
    ).reshape(n_fsdp, feature_width // n_fsdp, part_width)
    point_sent = point_part.astype(BF16)
    grad_point = tree_sum(
        [pick(point_part, f)]
        + [
            flip_fsdp(pick(point_sent, f ^ mask), mask).astype(F32)
            for mask in range(1, n_fsdp)
        ]
    )

    act_grad = lax.dot_general(
        grad_residual, full_panel, (((1,), (1,)), ((), ())), preferred_element_type=F32
    )
    normed_grad = act_grad * gate_sig * (1.0 + normed * (1.0 - gate_sig))
    gain_grad = jnp.sum(normed_grad * standard, axis=0)
    scaled = normed_grad * norm_gain
    conv_grad = inv_std * (
        scaled
        - jnp.mean(scaled, axis=1, keepdims=True)
        - standard * jnp.mean(scaled * standard, axis=1, keepdims=True)
    )
    kernel_grad = [jnp.sum(conv_grad * kept, axis=0) for kept in kept_list]
    grad_pad = jnp.pad(conv_grad, ((half_taps, half_taps), (0, 0)))
    glu_grad = jnp.zeros((row_count, feature_width), F32)
    for offset in range(tap_count):
        begin_row = 2 * half_taps - offset
        same_seg = (seg_pad[begin_row : begin_row + row_count] == segments)[:, None]
        glu_grad = glu_grad + conv_kernel[offset] * jnp.where(
            same_seg, grad_pad[begin_row : begin_row + row_count], 0.0
        )

    core = d & 1
    packet = jnp.stack(kernel_grad + [gain_grad]).reshape(2, -1, feature_width)
    packet = pick(packet, core) + flip_dp(pick(packet, 1 - core).astype(BF16), 1).astype(F32)
    packet = packet.astype(BF16)
    packet = tree_sum(
        [packet.astype(F32)]
        + [flip_dp(packet, mask).astype(F32) for mask in range(2, n_dp, 2)]
    )
    packet = packet.astype(BF16)
    packet = tree_sum(
        [packet.astype(F32)]
        + [flip_fsdp(packet, mask).astype(F32) for mask in range(1, n_fsdp)]
    )
    packet = ordered(core, packet, flip_dp(packet, 1), 0).reshape(-1, feature_width)

    loss_sum = loss_part.reshape(1, 1)
    for bit in range(n_dp.bit_length() - 1):
        loss_sum = loss_sum + flip_dp(loss_sum, 1 << bit)
    loss = loss_sum[0, 0] / (row_count * n_dp * n_fsdp)
    return (
        loss,
        grad_head,
        grad_point,
        packet[:tap_count],
        packet[tap_count],
        grad_residual,
        glu_grad.astype(BF16),
    )


def solution(mesh):
    placed = (
        P(("dp", "fsdp"), None),
        P(("dp", "fsdp"), None),
        P("dp", "fsdp", None, None),
        P("dp", "fsdp", None),
        P("dp", "fsdp", None),
        P("dp", None),
        P(),
        P(),
        P("fsdp", None),
        P(None, "fsdp"),
    )
    return jax.shard_map(
        local,
        mesh=mesh,
        in_specs=placed,
        out_specs=(
            P(),
            P("dp", "fsdp"),
            P("fsdp", "dp"),
            P(),
            P(),
            P(("dp", "fsdp"), None),
            P(("dp", "fsdp"), None),
        ),
        check_vma=False,
    )
```

time: 534 us -> 292 us (0.55)
  waiting for transfers between devices: 355 us -> 81.2 us
  blocking collectives: 63.6 us -> 0 us
  starting transfers between devices: 9.54 us -> 63.1 us
  local copies, waits for them, and re-layouts: 16.9 us -> 50.1 us
  other arithmetic: 31.3 us -> 46.4 us
  between operations: 19 us -> 6.8 us
    psum x1 -> x0, waiting for transfers between devices: 127 us -> none  [local(): lax.psum((loss_part, kernel_grad, gain_grad), ('dp', 'fsdp'))]
    reduce_scatter x3 -> x0, waiting for transfers between devices: 99 us -> none  [the longest x1 58.9 us: local(): lax.psum_scatter(lax.dot_general(logit_grad, code_head, (((1,), (1,)), ((...]
    all_gather x2 -> x0, waiting for transfers between devices: 85.5 us -> none  [the longest x1 50 us: local(): full_panel = lax.all_gather(point_weight, 'fsdp', axis=0, tiled=True)]
    ppermute x0 -> x38, waiting for transfers between devices: none -> 73.6 us  [the longest x20 37.8 us: flip_dp(): return lax.ppermute(value, 'dp', [(i, i ^ mask) for i in range(count)])]
    ppermute x0 -> x38, starting transfers between devices: none -> 52 us  [the longest x7 19.2 us: shift_fsdp(): lax.ppermute(value, 'fsdp', [(i, (i + step) % count) for i in range(count)])]
    psum x1 -> x0, blocking collectives: 39.9 us -> none  [local(): lax.psum((loss_part, kernel_grad, gain_grad), ('dp', 'fsdp'))]
    unnamed x8 -> x0, waiting for transfers between devices: 23.7 us -> none
    all_gather x2 -> x0, blocking collectives: 23.7 us -> none  [merged(): pieces = jax.tree.map(lambda part: lax.all_gather(part, axis), value)]
  transfers between devices with their start and end apart: 9 -> 41, of which waited for: 9 -> 20; matrix products, arithmetic and copies ran while one was open for 10% -> 43% of each run, Pallas kernels for 0% -> 0%
where the time goes in v1:
time: 292 us; the launch traced here: 287 us
  waiting for transfers between devices  81.2 us (28%)
  starting transfers between devices  63.1 us (22%)
  local copies, waits for them, and re-layouts  50.1 us (17%)
  other arithmetic  46.4 us (16%)
  matrix products  39.6 us (14%)
  between operations  6.8 us (2%)
    ppermute x20, waiting for transfers between devices, flip_dp(): return lax.ppermute(value, 'dp', [(i, i ^ mask) for i in range(count)])  37.8 us
    ppermute x7, waiting for transfers between devices, shift_fsdp(): lax.ppermute(value, 'fsdp', [(i, (i + step) % count) for i in range(count)])  33.4 us
    ppermute x7, starting transfers between devices, shift_fsdp(): lax.ppermute(value, 'fsdp', [(i, (i + step) % count) for i in range(count)])  19.2 us
    ppermute x20, starting transfers between devices, flip_dp(): return lax.ppermute(value, 'dp', [(i, i ^ mask) for i in range(count)])  18 us
    ppermute x9, starting transfers between devices, flip_fsdp(): return lax.ppermute(value, 'fsdp', [(i, i ^ mask) for i in range(count)])  13.9 us
    dot_general x4, matrix products, row_grad(): lax.dot_general(grads[distance], code_head, (((1,), (1,)), ((), ())), pre...  11.7 us
    dot_general x4, matrix products, local(): logits[distance] = jnp.dot(block, code_head, preferred_element_type=F32)  10.4 us
    unnamed x225, local copies, waits for them, and re-layouts  7.98 us
  transfers between devices with their start and end apart: 41, of which 20 were waited for; matrix products, arithmetic and copies ran while one was open for 43% of the time, Pallas kernels for 0%

profile of v1, /device:TPU:0, one launch (start us, length us, event | category | flops | bytes accessed | tf_op | source)
XLA Modules:
  0.0 287.1 jit_solution(13306423587980834527)
XLA Ops:
  11.5 3.7 %all-to-all-start.1 = ((bf16[8,32,1536]{2,1,0:T(8,128)(2,1)}), bf16[8,32,1536]{2,1,0:T(8,128)(2,1)S(1)}, u32[]{:S(2)}, u32[]{:S(2)}) async-start(bf16[8,32,1536]{2,1,0:T(8,128)(2,1)} %bitcast.6), calls=%async_computation.1 | async-start | bytes 1572864 | tf_op jit(solution)/shard_map/all_to_all | solution.py:138
  20.8 6.2 %collective-permute-done.1 = bf16[2,48,1536]{2,1,0:T(8,128)(2,1)S(1)} collective-permute-done((bf16[2,48,1536]{2,1,0:T(8,128)(2,1)S(1)}, bf16[2,48,1536]{2,1,0:T(8,128)(2,1)S(1)}, u32[]{:S(2)}, u32[]{:S(2)}) %collective-permute-start.1) | collective-permute-done | bytes 294944 | tf_op jit(solution)/shard_map/ppermute | solution.py:22
  31.2 3.7 %all-to-all-start = ((bf16[8,32,1536]{2,1,0:T(8,128)(2,1)}), bf16[8,32,1536]{2,1,0:T(8,128)(2,1)S(1)}, u32[]{:S(2)}, u32[]{:S(2)}) async-start(bf16[8,32,1536]{2,1,0:T(8,128)(2,1)} %bitcast.1), calls=%async_computation | async-start | bytes 1572864 | tf_op jit(solution)/shard_map/all_to_all | solution.py:141
  37.0 5.7 %fusion.207 = (f32[128]{0:T(128)}, f32[128,1536]{1,0:T(8,128)S(1)}) fusion(pred[128]{0:T(512)(128)(4,1)} %get-tuple-element.142, f32[1536]{0:T(1024)S(1)} %get-tuple-element.78, pred[128]{0:T(512)(128)(4,1)S(1)} %get-tuple-element.114, f32[1536]{0:T(1024)S(1)} %get-tuple-element.79, pred[128]{0:T(512)(128)(4,1)S(1)} %get-tuple-element.115, ...), kind=kLoop, calls=%fused_computation.472 | loop fusion | flops 18087808 | bytes 1767680 | tf_op jit(solution)/shard_map/reduce_sum | solution.py:155
  44.6 3.4 %fusion.205 = (bf16[3,2,2,1,48,1536]{5,4,3,2,1,0:T(8,128)(2,1)}, bf16[3,2,2,48,1536]{4,3,2,1,0:T(8,128)(2,1)}) fusion(bf16[3,1,2,48,1536]{4,3,2,1,0:T(8,128)(2,1)S(1)} %maximum_select_fusion.2, bf16[3,1,1,48,1536]{4,3,0,2,1:T(8,128)(2,1)} %bitcast.20, bf16[3,1,1,48,1536]{4,3,0,2,1:T(8,128)(2,1)S(1)} %get-tuple-element.96, pred[]{:T(512)S(6)} %eq.262), kind=kLoop, calls=%fused_computation.471 | loop fusion | flops 4866048 | bytes 5308417 | tf_op jit(solution)/shard_map/stack | solution.py:31
  61.9 9.3 %collective-permute-done.21 = bf16[128,1536]{1,0:T(8,128)(2,1)} collective-permute-done((bf16[128,1536]{1,0:T(8,128)(2,1)S(1)}, bf16[128,1536]{1,0:T(8,128)(2,1)}, u32[]{:S(2)}, u32[]{:S(2)}) %collective-permute-start.21) | collective-permute-done | bytes 393248 | tf_op jit(solution)/shard_map/ppermute | solution.py:12
  84.7 6.8 %collective-permute-start.6 = (bf16[128,1536]{1,0:T(8,128)(2,1)S(1)}, bf16[128,1536]{1,0:T(8,128)(2,1)S(1)}, u32[]{:S(2)}, u32[]{:S(2)}) collective-permute-start(bf16[128,1536]{1,0:T(8,128)(2,1)S(1)} %fusion.2), channel_id=1, source_target_pairs={{0,1},{1,2},{2,3},{3,0},{4,5},{5,6},{6,7},{7,4},{8,9},{9,10},{10,1... | collective-permute-start | bytes 1179656 | tf_op jit(solution)/shard_map/ppermute | solution.py:22
  96.6 5.9 %collective-permute-done.6 = bf16[128,1536]{1,0:T(8,128)(2,1)S(1)} collective-permute-done((bf16[128,1536]{1,0:T(8,128)(2,1)S(1)}, bf16[128,1536]{1,0:T(8,128)(2,1)S(1)}, u32[]{:S(2)}, u32[]{:S(2)}) %collective-permute-start.6) | collective-permute-done | bytes 393248 | tf_op jit(solution)/shard_map/ppermute | solution.py:22
  102.5 8.3 %collective-permute-done.7 = bf16[128,1536]{1,0:T(8,128)(2,1)} collective-permute-done((bf16[128,1536]{1,0:T(8,128)(2,1)S(1)}, bf16[128,1536]{1,0:T(8,128)(2,1)}, u32[]{:S(2)}, u32[]{:S(2)}) %collective-permute-start.7) | collective-permute-done | bytes 393248 | tf_op jit(solution)/shard_map/ppermute | solution.py:22
  112.5 4.2 %fusion.213 = (f32[128]{0:T(128)S(1)}, f32[128,2048]{1,0:T(8,128)S(1)}) fusion(bf16[128,1536]{1,0:T(8,128)(2,1)} %collective-permute-done.7, bf16[1536,2048]{1,0:T(8,128)(2,1)} %param.19), kind=kOutput, calls=%fused_computation.478 | convolution fusion | flops 805568384 | bytes 7733760 | tf_op jit(solution)/shard_map/dot_general | solution.py:171
  123.2 4.0 %fusion.214 = (f32[128]{0:T(128)S(1)}, f32[128,2048]{1,0:T(8,128)S(1)}) fusion(bf16[128,1536]{1,0:T(8,128)(2,1)} %collective-permute-done.8, bf16[1536,2048]{1,0:T(8,128)(2,1)} %param.19), kind=kOutput, calls=%fused_computation.479 | convolution fusion | flops 805568384 | bytes 7733760 | tf_op jit(solution)/shard_map/dot_general | solution.py:171
  144.1 5.1 %convolution_convert_fusion.1 = bf16[128,1536]{1,0:T(8,128)(2,1)S(1)} fusion(bf16[128,2048]{1,0:T(8,128)(2,1)S(1)} %subtract_convert_fusion, bf16[1536,2048]{1,0:T(8,128)(2,1)} %param.19), kind=kOutput, calls=%fused_computation.13 | convolution fusion | flops 805502976 | bytes 7208960 | tf_op jit(solution)/shard_map/dot_general | solution.py:200
  150.2 6.9 %convolution_convert_fusion = bf16[1536,2048]{1,0:T(8,128)(2,1)} fusion(bf16[128,2048]{1,0:T(8,128)(2,1)S(1)} %subtract_convert_fusion, bf16[128,2048]{1,0:T(8,128)(2,1)S(1)} %subtract_convert_fusion.1, bf16[128,2048]{1,0:T(8,128)(2,1)S(1)} %subtract_convert_fusion.2, bf16[128,2048]{1,0:T(8,128)(2,1)S(1)} %subtract_convert_fusion.3, ...), kind=kOutput, calls=%fused_computation.4 | convolution fusion | flops 3239051264 | bytes 9961472 | tf_op jit(solution)/shard_map/dot_general | solution.py:210
  168.0 7.4 %collective-permute-done.25 = bf16[128,1536]{1,0:T(8,128)(2,1)S(1)} collective-permute-done((bf16[128,1536]{1,0:T(8,128)(2,1)S(1)}, bf16[128,1536]{1,0:T(8,128)(2,1)S(1)}, u32[]{:S(2)}, u32[]{:S(2)}) %collective-permute-start.25) | collective-permute-done | bytes 393248 | tf_op jit(solution)/shard_map/ppermute | solution.py:22
  175.5 5.4 %collective-permute-done.26 = bf16[128,1536]{1,0:T(8,128)(2,1)S(1)} collective-permute-done((bf16[128,1536]{1,0:T(8,128)(2,1)S(1)}, bf16[128,1536]{1,0:T(8,128)(2,1)S(1)}, u32[]{:S(2)}, u32[]{:S(2)}) %collective-permute-start.26) | collective-permute-done | bytes 393248 | tf_op jit(solution)/shard_map/ppermute | solution.py:22
  181.2 4.3 %multiply_reduce_fusion = (f32[1536]{0:T(1024)S(1)}, f32[128]{0:T(128)S(1)}, f32[128]{0:T(128)S(1)}, f32[128,1536]{1,0:T(8,128)S(1)}) fusion(f32[128,1536]{1,0:T(8,128)S(1)} %get-tuple-element.86, f32[128]{0:T(128)S(1)} %copy-done.101, f32[128]{0:T(128)S(1)} %copy-done.92, f32[1536]{0:T(1024)S(1)} %copy-done.46, bf16[128,1536]{1,0:T(8,128)(2,1)S(1)} %fusion.22, ...), kind=kOutput, calls=%fused_computation.249 | convolution fusion | flops 607320320 | bytes 6699008 | tf_op jit(solution)/shard_map/dot_general | solution.py:245
  193.1 4.0 %dynamic-slice_bitcast_fusion = bf16[2,2,192,2048]{3,2,1,0:T(8,128)(2,1)} fusion(bf16[2,2,2,192,2048]{4,3,2,1,0:T(8,128)(2,1)} %bitcast.236, s32[]{:T(128)S(6)} %select_n.524), kind=kLoop, calls=%fused_computation.8 | loop fusion | bytes 6291460 | tf_op jit(solution)/shard_map/jit(dynamic_index_in_dim)/squeeze | solution.py:26
  211.9 4.8 %copy.49 = bf16[1536,1024]{1,0:T(8,128)(2,1)} copy(bf16[1536,1024]{0,1:T(8,128)(2,1)} %bitcast.77) | data formatting | bytes 6291456 | tf_op jit(solution)/shard_map/dot_general | solution.py:230
  228.4 5.4 %fusion.133 = bf16[128,1536]{1,0:T(8,128)(2,1)} fusion(f32[128,1536]{1,0:T(8,128)S(1)} %get-tuple-element.80, f32[1536]{0:T(1024)S(1)} %copy-done.42, f32[1536]{0:T(1024)S(1)} %copy-done.44, f32[1536]{0:T(1024)S(1)} %get-tuple-element.50, f32[1536]{0:T(1024)S(1)} %get-tuple-element.51, f32[1536]{0:T(1024)S(1)} %get-tuple-element.52, ...), kind=kLoop, calls=%fused_computation.232 | loop fusion | flops 18087936 | bytes 1373952 | tf_op jit(solution)/shard_map/convert_element_type | solution.py:292
  234.7 3.6 %all-to-all-start.2 = ((bf16[8,128,192]{1,2,0:T(8,128)(2,1)}), bf16[8,128,192]{1,2,0:T(8,128)(2,1)S(1)}, u32[]{:S(2)}, u32[]{:S(2)}) async-start(bf16[8,128,192]{1,2,0:T(8,128)(2,1)} %bitcast.80), calls=%async_computation.2 | async-start | bytes 786432 | tf_op jit(solution)/shard_map/all_to_all | solution.py:216
  239.0 7.6 %all-to-all-done.2 = bf16[8,128,192]{1,2,0:T(8,128)(2,1)S(1)} async-done(((bf16[8,128,192]{1,2,0:T(8,128)(2,1)}), bf16[8,128,192]{1,2,0:T(8,128)(2,1)S(1)}, u32[]{:S(2)}, u32[]{:S(2)}) %all-to-all-start.2) | async-done | bytes 393248 | tf_op jit(solution)/shard_map/all_to_all | solution.py:216
  246.8 4.2 %fusion = bf16[2,2,192,2048]{3,2,1,0:T(8,128)(2,1)S(1)} fusion(bf16[2,2,192,2048]{3,2,1,0:T(8,128)(2,1)} %collective-permute-done.15, bf16[2,2,2,192,2048]{4,3,2,1,0:T(8,128)(2,1)} %bitcast.237, s32[]{:T(128)S(6)} %select_n.523), kind=kLoop, calls=%fused_computation.6 | loop fusion | flops 6291456 | bytes 9437188 | tf_op jit(solution)/shard_map/convert_element_type | solution.py:107
  263.1 8.8 %collective-permute-done.16 = bf16[2,192,1024]{2,1,0:T(8,128)(2,1)S(1)} collective-permute-done((bf16[2,192,1024]{2,1,0:T(8,128)(2,1)}, bf16[2,192,1024]{2,1,0:T(8,128)(2,1)S(1)}, u32[]{:S(2)}, u32[]{:S(2)}) %collective-permute-start.16) | collective-permute-done | bytes 786464 | tf_op jit(solution)/shard_map/ppermute | solution.py:12
  275.8 6.7 %collective-permute-done.17 = bf16[192,1024]{1,0:T(8,128)(2,1)S(1)} collective-permute-done((bf16[192,1024]{1,0:T(8,128)(2,1)S(1)}, bf16[192,1024]{1,0:T(8,128)(2,1)S(1)}, u32[]{:S(2)}, u32[]{:S(2)}) %collective-permute-start.17) | collective-permute-done | bytes 393248 | tf_op jit(solution)/shard_map/ppermute | solution.py:12
  (427 shorter events, 144.9 us)
Async XLA Ops:
  2.2 18.6 %collective-permute-start = (bf16[2,48,1536]{2,1,0:T(8,128)(2,1)S(1)}, bf16[2,48,1536]{2,1,0:T(8,128)(2,1)S(1)}, u32[]{:S(2)}, u32[]{:S(2)}) collective-permute-start(bf16[2,48,1536]{2,1,0:T(8,128)(2,1)S(1)} %pad_maximum_fusion.4), channel_id=1, source_target_pairs={{0,1},{1,2},{2,3},{3,0},{4,5},{5,6},{6,7},{7,4},{8,9},{9,10},{10,1... | collective-permute-start | bytes 884744 | tf_op jit(solution)/shard_map/ppermute | solution.py:22
  5.2 21.8 %collective-permute-start.1 = (bf16[2,48,1536]{2,1,0:T(8,128)(2,1)S(1)}, bf16[2,48,1536]{2,1,0:T(8,128)(2,1)S(1)}, u32[]{:S(2)}, u32[]{:S(2)}) collective-permute-start(bf16[2,48,1536]{2,1,0:T(8,128)(2,1)S(1)} %pad_maximum_fusion.4), channel_id=1, source_target_pairs={{0,2},{1,3},{2,0},{3,1},{4,6},{5,7},{6,4},{7,5},{8,10},{9,11},{10,... | collective-permute-start | bytes 884744 | tf_op jit(solution)/shard_map/ppermute | solution.py:22
  7.8 19.2 %collective-permute-start.2 = (bf16[2,48,1536]{2,1,0:T(8,128)(2,1)S(1)}, bf16[2,48,1536]{2,1,0:T(8,128)(2,1)S(1)}, u32[]{:S(2)}, u32[]{:S(2)}) collective-permute-start(bf16[2,48,1536]{2,1,0:T(8,128)(2,1)S(1)} %pad_maximum_fusion.4), channel_id=1, source_target_pairs={{0,3},{1,0},{2,1},{3,2},{4,7},{5,4},{6,5},{7,6},{8,11},{9,8},{10,9... | collective-permute-start | bytes 884744 | tf_op jit(solution)/shard_map/ppermute | solution.py:22
  11.5 19.8 %all-to-all-start.1 = ((bf16[8,32,1536]{2,1,0:T(8,128)(2,1)}), bf16[8,32,1536]{2,1,0:T(8,128)(2,1)S(1)}, u32[]{:S(2)}, u32[]{:S(2)}) async-start(bf16[8,32,1536]{2,1,0:T(8,128)(2,1)} %bitcast.6), calls=%async_computation.1 | async-start | bytes 1572864 | tf_op jit(solution)/shard_map/all_to_all | solution.py:138
  28.2 15.1 %collective-permute-start.4 = (bf16[3,48,1536]{2,1,0:T(8,128)(2,1)}, bf16[3,48,1536]{2,1,0:T(8,128)(2,1)}, u32[]{:S(2)}, u32[]{:S(2)}) collective-permute-start(bf16[3,48,1536]{2,1,0:T(8,128)(2,1)} %get-tuple-element.98), channel_id=1, source_target_pairs={{0,16},{4,20},{8,24},{12,28},{16,0},{20,4},{24,8},{28,12},{1,17},{... | collective-permute-start | bytes 1327112 | tf_op jit(solution)/shard_map/ppermute | solution.py:12
  29.8 14.9 %collective-permute-start.3 = (bf16[3,48,1536]{2,1,0:T(8,128)(2,1)}, bf16[3,48,1536]{2,1,0:T(8,128)(2,1)}, u32[]{:S(2)}, u32[]{:S(2)}) collective-permute-start(bf16[3,48,1536]{2,1,0:T(8,128)(2,1)} %get-tuple-element.97), channel_id=1, source_target_pairs={{0,8},{4,12},{8,0},{12,4},{16,24},{20,28},{24,16},{28,20},{1,9},{5... | collective-permute-start | bytes 1327112 | tf_op jit(solution)/shard_map/ppermute | solution.py:12
  31.2 25.8 %all-to-all-start = ((bf16[8,32,1536]{2,1,0:T(8,128)(2,1)}), bf16[8,32,1536]{2,1,0:T(8,128)(2,1)S(1)}, u32[]{:S(2)}, u32[]{:S(2)}) async-start(bf16[8,32,1536]{2,1,0:T(8,128)(2,1)} %bitcast.1), calls=%async_computation | async-start | bytes 1572864 | tf_op jit(solution)/shard_map/all_to_all | solution.py:141
  48.1 27.4 %collective-permute-start.5 = (bf16[3,2,2,48,1536]{4,3,2,1,0:T(8,128)(2,1)}, bf16[3,2,2,48,1536]{4,3,2,1,0:T(8,128)(2,1)}, u32[]{:S(2)}, u32[]{:S(2)}) collective-permute-start(bf16[3,2,2,48,1536]{4,3,2,1,0:T(8,128)(2,1)} %get-tuple-element.93), channel_id=1, source_target_pairs={{0,4},{4,0},{8,12},{12,8},{16,20},{20,16},{24,28},{28,24},{1,5},{5... | collective-permute-start | bytes 5308424 | tf_op jit(solution)/shard_map/ppermute | solution.py:12
  51.5 19.6 %collective-permute-start.21 = (bf16[128,1536]{1,0:T(8,128)(2,1)S(1)}, bf16[128,1536]{1,0:T(8,128)(2,1)}, u32[]{:S(2)}, u32[]{:S(2)}) collective-permute-start(bf16[128,1536]{1,0:T(8,128)(2,1)S(1)} %get-tuple-element.82), channel_id=1, source_target_pairs={{0,16},{4,20},{8,24},{12,28},{16,0},{20,4},{24,8},{28,12},{1,17},{... | collective-permute-start | bytes 1179656 | tf_op jit(solution)/shard_map/ppermute | solution.py:12
  53.0 18.1 %collective-permute-start.22 = (bf16[128,1536]{1,0:T(8,128)(2,1)S(1)}, bf16[128,1536]{1,0:T(8,128)(2,1)S(1)}, u32[]{:S(2)}, u32[]{:S(2)}) collective-permute-start(bf16[128,1536]{1,0:T(8,128)(2,1)S(1)} %get-tuple-element.82), channel_id=1, source_target_pairs={{0,24},{4,28},{8,16},{12,20},{16,8},{20,12},{24,0},{28,4},{1,25},{... | collective-permute-start | bytes 1179656 | tf_op jit(solution)/shard_map/ppermute | solution.py:12
  73.7 135.5 %collective-permute-start.23 = (bf16[512,1536]{1,0:T(8,128)(2,1)}, bf16[512,1536]{1,0:T(8,128)(2,1)}, u32[]{:S(2)}, u32[]{:S(2)}) collective-permute-start(bf16[512,1536]{1,0:T(8,128)(2,1)} %pad_maximum_fusion.2), channel_id=1, source_target_pairs={{0,4},{4,0},{8,12},{12,8},{16,20},{20,16},{24,28},{28,24},{1,5},{5... | collective-permute-start | bytes 4718600 | tf_op jit(solution)/shard_map/ppermute | solution.py:12
  84.7 17.9 %collective-permute-start.6 = (bf16[128,1536]{1,0:T(8,128)(2,1)S(1)}, bf16[128,1536]{1,0:T(8,128)(2,1)S(1)}, u32[]{:S(2)}, u32[]{:S(2)}) collective-permute-start(bf16[128,1536]{1,0:T(8,128)(2,1)S(1)} %fusion.2), channel_id=1, source_target_pairs={{0,1},{1,2},{2,3},{3,0},{4,5},{5,6},{6,7},{7,4},{8,9},{9,10},{10,1... | collective-permute-start | bytes 1179656 | tf_op jit(solution)/shard_map/ppermute | solution.py:22
  91.5 19.4 %collective-permute-start.7 = (bf16[128,1536]{1,0:T(8,128)(2,1)S(1)}, bf16[128,1536]{1,0:T(8,128)(2,1)}, u32[]{:S(2)}, u32[]{:S(2)}) collective-permute-start(bf16[128,1536]{1,0:T(8,128)(2,1)S(1)} %fusion.2), channel_id=1, source_target_pairs={{0,3},{1,0},{2,1},{3,2},{4,7},{5,4},{6,5},{7,6},{8,11},{9,8},{10,9... | collective-permute-start | bytes 1179656 | tf_op jit(solution)/shard_map/ppermute | solution.py:22
  161.6 13.9 %collective-permute-start.25 = (bf16[128,1536]{1,0:T(8,128)(2,1)S(1)}, bf16[128,1536]{1,0:T(8,128)(2,1)S(1)}, u32[]{:S(2)}, u32[]{:S(2)}) collective-permute-start(bf16[128,1536]{1,0:T(8,128)(2,1)S(1)} %get-tuple-element.103), channel_id=1, source_target_pairs={{0,1},{1,2},{2,3},{3,0},{4,5},{5,6},{6,7},{7,4},{8,9},{9,10},{10,1... | collective-permute-start | bytes 1179656 | tf_op jit(solution)/shard_map/ppermute | solution.py:22
  163.9 17.0 %collective-permute-start.26 = (bf16[128,1536]{1,0:T(8,128)(2,1)S(1)}, bf16[128,1536]{1,0:T(8,128)(2,1)S(1)}, u32[]{:S(2)}, u32[]{:S(2)}) collective-permute-start(bf16[128,1536]{1,0:T(8,128)(2,1)S(1)} %get-tuple-element.104), channel_id=1, source_target_pairs={{0,3},{1,0},{2,1},{3,2},{4,7},{5,4},{6,5},{7,6},{8,11},{9,8},{10,9... | collective-permute-start | bytes 1179656 | tf_op jit(solution)/shard_map/ppermute | solution.py:22
  197.0 49.7 %collective-permute-start.15 = (bf16[2,2,192,2048]{3,2,1,0:T(8,128)(2,1)}, bf16[2,2,192,2048]{3,2,1,0:T(8,128)(2,1)}, u32[]{:S(2)}, u32[]{:S(2)}) collective-permute-start(bf16[2,2,192,2048]{3,2,1,0:T(8,128)(2,1)} %dynamic-slice_bitcast_fusion), channel_id=1, source_target_pairs={{0,4},{4,0},{8,12},{12,8},{16,20},{20,16},{24,28},{28,24},{1,5},{5... | collective-permute-start | bytes 9437192 | tf_op jit(solution)/shard_map/ppermute | solution.py:12
  204.7 23.4 %collective-permute-start.34 = (bf16[16,1536]{1,0:T(8,128)(2,1)S(1)}, bf16[16,1536]{1,0:T(8,128)(2,1)S(1)}, u32[]{:S(2)}, u32[]{:S(2)}) collective-permute-start(bf16[16,1536]{1,0:T(8,128)(2,1)S(1)} %add_convert_fusion), channel_id=1, source_target_pairs={{0,1},{1,0},{2,3},{3,2},{4,5},{5,4},{6,7},{7,6},{8,9},{9,8},{10,11... | collective-permute-start | bytes 147464 | tf_op jit(solution)/shard_map/ppermute | solution.py:17
  205.3 22.8 %collective-permute-start.35 = (bf16[16,1536]{1,0:T(8,128)(2,1)S(1)}, bf16[16,1536]{1,0:T(8,128)(2,1)S(1)}, u32[]{:S(2)}, u32[]{:S(2)}) collective-permute-start(bf16[16,1536]{1,0:T(8,128)(2,1)S(1)} %add_convert_fusion), channel_id=1, source_target_pairs={{0,2},{1,3},{2,0},{3,1},{4,6},{5,7},{6,4},{7,5},{8,10},{9,11},{10,... | collective-permute-start | bytes 147464 | tf_op jit(solution)/shard_map/ppermute | solution.py:17
  207.1 21.0 %collective-permute-start.36 = (bf16[16,1536]{1,0:T(8,128)(2,1)S(1)}, bf16[16,1536]{1,0:T(8,128)(2,1)S(1)}, u32[]{:S(2)}, u32[]{:S(2)}) collective-permute-start(bf16[16,1536]{1,0:T(8,128)(2,1)S(1)} %add_convert_fusion), channel_id=1, source_target_pairs={{0,3},{1,2},{2,1},{3,0},{4,7},{5,6},{6,5},{7,4},{8,11},{9,10},{10,... | collective-permute-start | bytes 147464 | tf_op jit(solution)/shard_map/ppermute | solution.py:17
  253.3 18.5 %collective-permute-start.16 = (bf16[2,192,1024]{2,1,0:T(8,128)(2,1)}, bf16[2,192,1024]{2,1,0:T(8,128)(2,1)S(1)}, u32[]{:S(2)}, u32[]{:S(2)}) collective-permute-start(bf16[2,192,1024]{2,1,0:T(8,128)(2,1)} %dynamic-slice_bitcast_fusion.2), channel_id=1, source_target_pairs={{0,8},{4,12},{8,0},{12,4},{16,24},{20,28},{24,16},{28,20},{1,9},{5... | collective-permute-start | bytes 2359304 | tf_op jit(solution)/shard_map/ppermute | solution.py:12
  254.7 19.8 %collective-permute-start.18 = (bf16[2,192,1024]{2,1,0:T(8,128)(2,1)S(1)}, bf16[2,192,1024]{2,1,0:T(8,128)(2,1)S(1)}, u32[]{:S(2)}, u32[]{:S(2)}) collective-permute-start(bf16[2,192,1024]{2,1,0:T(8,128)(2,1)S(1)} %dynamic-slice_bitcast_fusion.1), channel_id=1, source_target_pairs={{0,16},{4,20},{8,24},{12,28},{16,0},{20,4},{24,8},{28,12},{1,17},{... | collective-permute-start | bytes 2359304 | tf_op jit(solution)/shard_map/ppermute | solution.py:12
  258.6 16.3 %collective-permute-start.27 = (bf16[384,192]{0,1:T(8,128)(2,1)S(1)}, bf16[384,192]{0,1:T(8,128)(2,1)S(1)}, u32[]{:S(2)}, u32[]{:S(2)}) collective-permute-start(bf16[384,192]{0,1:T(8,128)(2,1)S(1)} %get-tuple-element.100), channel_id=1, source_target_pairs={{0,1},{1,0},{2,3},{3,2},{4,5},{5,4},{6,7},{7,6},{8,9},{9,8},{10,11... | collective-permute-start | bytes 442376 | tf_op jit(solution)/shard_map/ppermute | solution.py:17
  258.7 16.3 %collective-permute-start.28 = (bf16[384,192]{0,1:T(8,128)(2,1)S(1)}, bf16[384,192]{0,1:T(8,128)(2,1)S(1)}, u32[]{:S(2)}, u32[]{:S(2)}) collective-permute-start(bf16[384,192]{0,1:T(8,128)(2,1)S(1)} %get-tuple-element.102), channel_id=1, source_target_pairs={{0,2},{1,3},{2,0},{3,1},{4,6},{5,7},{6,4},{7,5},{8,10},{9,11},{10,... | collective-permute-start | bytes 442376 | tf_op jit(solution)/shard_map/ppermute | solution.py:17
  261.1 13.9 %collective-permute-start.29 = (bf16[384,192]{0,1:T(8,128)(2,1)S(1)}, bf16[384,192]{0,1:T(8,128)(2,1)S(1)}, u32[]{:S(2)}, u32[]{:S(2)}) collective-permute-start(bf16[384,192]{0,1:T(8,128)(2,1)S(1)} %get-tuple-element.101), channel_id=1, source_target_pairs={{0,3},{1,2},{2,1},{3,0},{4,7},{5,6},{6,5},{7,4},{8,11},{9,10},{10,... | collective-permute-start | bytes 442376 | tf_op jit(solution)/shard_map/ppermute | solution.py:17
  (128 other events, 1293.3 us)
